TPU v7x, 128 devices: a whole 4x4x4 slice. The times are simulated.
128 devices in a mesh: oct: 2 (over core), sub: 64 (over x, z, y).
Axes of the slice: x: 4, y: 4, z: 4, core: 2. Of those that a mesh axis runs over, the one named last changes fastest.
Arguments:
- coefficients: float32 [2048, 4096], P(('oct', 'sub')), may hold values from -6 to 6
- potential: float32 [2048, 4096], P(('oct', 'sub')), may hold values from 0.2 to 2
- to_values: float32 [16, 16], replicated, may hold values from -1.5 to 1.5
- x_kernels: bfloat16 [20, 48, 16], replicated, may hold values from -0.5 to 0.5
- yz_kernels: bfloat16 [256, 46080], replicated, may hold values from -0.046875 to 0.046875
- two_scale: float32 [2, 16, 16], replicated, may hold values from -1 to 1
- disp_ids: int32 [2048, 16], P(('oct', 'sub')), may hold values from -1 to 26, as said below
- dest_box: int32 [2048, 16], P(('oct', 'sub')), may hold values from -1 to 2047, as said below
- parent_of: int32 [2048], P(('oct', 'sub')), may hold values from 0 to 255, as said below
- child_octant: int32 [2048], P(('oct', 'sub')), may hold values from 0 to 7
Outputs:
- next_field: float32 [2048, 4096], P(('oct', 'sub'))
- parents: float32 [256, 4096], P(('oct', 'sub'))
Inputs may be any that keep to these rules, and one draw needn't show every extreme that they name: `disp_ids`: -1 marks an empty slot, exactly where dest_box is -1; in every row the live slots come first, 4 or more of them. `dest_box`: among the live slots of one aligned block of 16 rows, at most 2 name boxes of any one aligned block of 16 boxes; some box block receives exactly 2 from every row block. Every parent is named by exactly 8 boxes, whose child_octant values are 0 to 7; parent_of[b] // 128 == b // 1024. Within one aligned block of 16 boxes, at most 1 box has its parent in any one aligned block of 2 parents, and some parent block is named by exactly 1 of them.
All inputs are finite; a program needn't handle non-finite values.
Results may differ from a plain program's by a relative error of at most 0.018.
Values may be sent and summed in bfloat16 or wider, within the bound.
A program may use at most 192 MiB of HBM per device.

v0:
```python
import jax
import jax.numpy as jnp
from jax import lax
from jax.sharding import PartitionSpec as P

ITERS = 2


def apply_pair(blocks, along_x, pair, order_k):
    highest = lax.Precision.HIGHEST
    rows_total = blocks.shape[0]
    plane_size = order_k * order_k
    inner = jnp.dot(blocks.reshape(rows_total * order_k, plane_size), pair, precision=highest)
    inner = inner.reshape(rows_total, order_k, plane_size)
    return jnp.einsum("ix,bxr->bir", along_x, inner, precision=highest).reshape(
        rows_total, plane_size * order_k
    )


def quad_of(filters):
    order_k = filters.shape[1]
    return jnp.einsum("cjy,dkz->yzcdjk", filters, filters, precision=lax.Precision.HIGHEST).reshape(
        order_k * order_k, 4 * order_k * order_k
    )


def lift_boxes(blocks, filters, quad, octant):
    highest = lax.Precision.HIGHEST
    rows_total = blocks.shape[0]
    order_k = filters.shape[1]
    plane_size = order_k * order_k
    inner = jnp.dot(blocks.reshape(rows_total * order_k, plane_size), quad, precision=highest)
    inner = inner.reshape(rows_total, order_k, 4, plane_size)
    select = (octant[:, None] % 4 == jnp.arange(4)[None, :]).astype(jnp.float32)
    inner = jnp.einsum("bxcr,bc->bxr", inner, select, precision=highest)
    along_x = jnp.where((octant // 4 == 1)[:, None, None], filters[1][None], filters[0][None])
    return jnp.einsum("bix,bxr->bir", along_x, inner, precision=highest).reshape(
        rows_total, plane_size * order_k
    )


def shards(
    coefficients,
    potential,
    to_values,
    x_kernels,
    yz_kernels,
    two_scale,
    disp_ids,
    dest_box,
    parent_of,
    child_octant,
):
    highest = lax.Precision.HIGHEST
    box_count = coefficients.shape[0]
    order_k = to_values.shape[0]
    plane_size = order_k * order_k
    cube_size = plane_size * order_k
    slot_count = disp_ids.shape[1]
    term_count = x_kernels.shape[0]
    oct_count = lax.axis_size("oct")
    sub_count = lax.axis_size("sub")
    devices_all = oct_count * sub_count
    capacity = box_count * slot_count // devices_all
    block_boxes = 16
    count_blocks = box_count // block_boxes
    parent_local = box_count // 8
    per_group = sub_count * parent_local
    value_pair = jnp.einsum("jy,kz->yzjk", to_values, to_values, precision=highest).reshape(
        plane_size, plane_size
    )
    back_pair = jnp.einsum("yj,zk->yzjk", to_values, to_values, precision=highest).reshape(
        plane_size, plane_size
    )
    flipped = jnp.swapaxes(two_scale, 1, 2)
    lift_quad = quad_of(two_scale)
    drop_quad = quad_of(flipped)
    flat_dest = dest_box.reshape(-1)
    owner_ids = flat_dest // box_count
    is_live = flat_dest >= 0
    hits = (owner_ids[:, None] == jnp.arange(devices_all, dtype=jnp.int32)[None, :]).astype(
        jnp.int32
    )
    before = jnp.cumsum(hits, axis=0) - hits
    rank_ids = jnp.sum(before * hits, axis=1)
    slot_index = jnp.where(is_live, owner_ids * capacity + rank_ids, devices_all * capacity)
    local_box = flat_dest - owner_ids * box_count
    label_row = (
        jnp.zeros((devices_all * capacity + 1,), jnp.bfloat16)
        .at[slot_index]
        .set(local_box.astype(jnp.bfloat16))[:-1]
    )
    local_parents = parent_of - lax.axis_index("oct") * per_group
    member_up = (jnp.arange(per_group, dtype=jnp.int32)[:, None] == local_parents[None, :]).astype(
        jnp.float32
    )
    box_ids = jnp.arange(box_count, dtype=jnp.int32)

    def convolve(carry_none, block_items):
        source_blk, disp_blk = block_items
        partial_value = jnp.dot(
            source_blk.reshape(block_boxes * order_k, plane_size),
            yz_kernels,
            preferred_element_type=jnp.float32,
        ).astype(jnp.bfloat16)
        partial_value = partial_value.reshape(block_boxes, order_k, term_count, 9 * plane_size)
        convolved = jnp.einsum(
            "bxmr,max->bar", partial_value, x_kernels, preferred_element_type=jnp.float32
        )
        convolved = (
            convolved.reshape(block_boxes, 3, order_k, 9, plane_size)
            .transpose(0, 1, 3, 2, 4)
            .reshape(block_boxes, 27, cube_size)
        )
        picked = jnp.take_along_axis(
            convolved, jnp.maximum(disp_blk, 0)[:, :, None], axis=1
        ).astype(jnp.bfloat16)
        return (carry_none, picked)

    current = coefficients
    own_parents = jnp.zeros((parent_local, cube_size), jnp.float32)
    for iteration in range(ITERS):
        values = apply_pair(current, to_values, value_pair, order_k)
        product = values * (potential + 0.25 * values * values)
        source = apply_pair(product, to_values.T, back_pair, order_k).astype(jnp.bfloat16)
        unused, picked = lax.scan(
            convolve,
            jnp.zeros((), jnp.int32),
            (
                source.reshape(count_blocks, block_boxes, cube_size),
                disp_ids.reshape(count_blocks, block_boxes, slot_count),
            ),
        )
        outgoing = picked.reshape(box_count * slot_count, cube_size)
        send_tiles = (
            jnp.zeros((devices_all * capacity + 1, cube_size), jnp.bfloat16)
            .at[slot_index]
            .set(outgoing)[:-1]
        )
        arrived, arrived_labels = (
            lax.all_to_all(
                send_tiles.reshape(devices_all, capacity, cube_size),
                ("oct", "sub"),
                split_axis=0,
                concat_axis=0,
                tiled=True,
            ),
            lax.all_to_all(
                label_row.reshape(devices_all, capacity),
                ("oct", "sub"),
                split_axis=0,
                concat_axis=0,
                tiled=True,
            ),
        )
        incoming = arrived.reshape(devices_all * capacity, cube_size)
        arrived_boxes = arrived_labels.reshape(-1).astype(jnp.int32)
        member_in = (arrived_boxes[None, :] == box_ids[:, None]).astype(jnp.bfloat16)
        gathered = jnp.dot(member_in, incoming, preferred_element_type=jnp.float32)
        lifted = lift_boxes(gathered, two_scale, lift_quad, child_octant)
        contrib = jnp.dot(member_up, lifted, precision=highest)
        own_parents = lax.psum_scatter(contrib, "sub", scatter_dimension=0, tiled=True)
        everyone = lax.all_gather(
            own_parents.astype(jnp.bfloat16), "sub", axis=0, tiled=True
        ).astype(own_parents.dtype)
        matched = jnp.take(everyone, local_parents, axis=0)
        current = gathered - lift_boxes(matched, flipped, drop_quad, child_octant)
    return (current, own_parents)


def solution(mesh):
    placed = (
        P(("oct", "sub"), None),
        P(("oct", "sub"), None),
        P(),
        P(),
        P(),
        P(),
        P(("oct", "sub"), None),
        P(("oct", "sub"), None),
        P(("oct", "sub")),
        P(("oct", "sub")),
    )
    return jax.shard_map(
        shards,
        mesh=mesh,
        in_specs=placed,
        out_specs=(P(("oct", "sub"), None), P(("oct", "sub"), None)),
        check_vma=False,
    )
```

profile of v0, /device:TPU:0, one launch (start us, length us, event | category | flops | bytes accessed | tf_op | source)
XLA Modules:
  0.0 983.5 jit_solution(8387002277231726505)
XLA Ops:
  13.1 11.9 %all-to-all-start = ((bf16[128,1,2]{2,1,0:T(2,128)(2,1)}), bf16[128,1,2]{2,1,0:T(2,128)(2,1)}, u32[]{:S(2)}, u32[]{:S(2)}) async-start(bf16[128,1,2]{2,1,0:T(2,128)(2,1)} %all_to_all.17), calls=%async_computation | async-start | bytes 131072 | tf_op jit(solution)/shard_map/all_to_all | solution.py:148
  35.0 20.6 %convolution_convert_fusion.1 = bf16[256,46080]{1,0:T(8,128)(2,1)} fusion(bf16[256,256]{1,0:T(8,128)(2,1)S(1)} %bitcast.221, bf16[256,46080]{1,0:T(8,128)(2,1)} %param.18), kind=kOutput, calls=%fused_computation.8 | convolution fusion | flops 6051594240 | bytes 47316992 | tf_op jit(solution)/shard_map/while/body/eval_jaxpr/dot_general | solution.py:101
  55.6 32.9 %reshape.316 = bf16[16,16,20,2304]{3,2,1,0:T(8,128)(2,1)} reshape(bf16[256,46080]{1,0:T(8,128)(2,1)} %convolution_convert_fusion.1) | data formatting | bytes 47185920 | tf_op jit(solution)/shard_map/while/body/eval_jaxpr/reshape | solution.py:106
  88.5 11.5 %convolution_bitcast_fusion.1 = bf16[16,48,2304]{2,1,0:T(8,128)(2,1)S(1)} fusion(bf16[16,16,20,2304]{3,2,1,0:T(8,128)(2,1)} %reshape.316, bf16[20,48,16]{1,2,0:T(8,128)(2,1)} %param.17), kind=kOutput, calls=%fused_computation.12 | convolution fusion | flops 1132462080 | bytes 27162624 | tf_op jit(solution)/shard_map/while/body/eval_jaxpr/bxmr,max->bar/dot_general | solution.py:107
  104.9 6.0 copy.44
  110.9 5.4 reshape.318
  117.1 8.5 gather_fusion
  140.2 9.9 %all-to-all-start.1 = ((bf16[128,2,4096]{2,1,0:T(2,128)(2,1)}), bf16[128,2,4096]{2,1,0:T(2,128)(2,1)S(1)}, u32[]{:S(2)}, u32[]{:S(2)}) async-start(bf16[128,2,4096]{2,1,0:T(2,128)(2,1)} %reshape.320), calls=%async_computation.1 | async-start | bytes 4194304 | tf_op jit(solution)/shard_map/all_to_all | solution.py:141
  154.6 8.7 reshape.322
  167.7 12.3 %all-to-all-done.1 = bf16[128,2,4096]{2,1,0:T(2,128)(2,1)S(1)} async-done(((bf16[128,2,4096]{2,1,0:T(2,128)(2,1)}), bf16[128,2,4096]{2,1,0:T(2,128)(2,1)S(1)}, u32[]{:S(2)}, u32[]{:S(2)}) %all-to-all-start.1) | async-done | bytes 2097184 | tf_op jit(solution)/shard_map/all_to_all | solution.py:141
  188.6 366.1 %all-reduce.6 = bf16[128,4096]{1,0:T(8,128)(2,1)S(1)} all-reduce(f32[128,4096]{1,0:T(8,128)S(1)} %fusion.55), channel_id=2, replica_groups=mesh['oct'=2,'sub'=64] {'sub'}, use_global_device_ids=true, to_apply=%region_5.7.clone | all-reduce | flops 524288 | bytes 3145728
  559.8 8.0 reshape.324
  568.4 45.9 %all-gather.5.cloned.1.call-done = bf16[64,2,4096]{2,1,0:T(2,128)(2,1)} async-done(((bf16[1,2,4096]{2,1,0:T(2,128)(2,1)}), bf16[64,2,4096]{2,1,0:T(2,128)(2,1)}) %all-gather.5.cloned.1.call-update) | async-done | bytes 1048592 | tf_op jit(solution)/shard_map/all_gather | solution.py:163
  623.5 20.6 %convolution_convert_fusion = bf16[256,46080]{1,0:T(8,128)(2,1)} fusion(bf16[256,256]{1,0:T(8,128)(2,1)S(1)} %bitcast.222, bf16[256,46080]{1,0:T(8,128)(2,1)} %param.18), kind=kOutput, calls=%fused_computation.7 | convolution fusion | flops 6051594240 | bytes 47316992 | tf_op jit(solution)/shard_map/while/body/eval_jaxpr/dot_general | solution.py:101
  644.1 32.9 %reshape.327 = bf16[16,16,20,2304]{3,2,1,0:T(8,128)(2,1)} reshape(bf16[256,46080]{1,0:T(8,128)(2,1)} %convolution_convert_fusion) | data formatting | bytes 47185920 | tf_op jit(solution)/shard_map/while/body/eval_jaxpr/reshape | solution.py:106
  677.0 11.5 %convolution_bitcast_fusion = bf16[16,48,2304]{2,1,0:T(8,128)(2,1)S(1)} fusion(bf16[16,16,20,2304]{3,2,1,0:T(8,128)(2,1)} %reshape.327, bf16[20,48,16]{1,2,0:T(8,128)(2,1)} %param.17), kind=kOutput, calls=%fused_computation.11 | convolution fusion | flops 1132462080 | bytes 27162624 | tf_op jit(solution)/shard_map/while/body/eval_jaxpr/bxmr,max->bar/dot_general | solution.py:107
  688.6 5.1 reshape.328
  693.7 6.0 copy.55
  699.7 5.1 reshape.329
  704.8 8.5 gather_fusion.2
  716.8 5.3 scatter_custom_fusion.2
  726.8 36.1 %all_to_all.21 = bf16[128,2,4096]{2,1,0:T(2,128)(2,1)} all-to-all(bf16[128,2,4096]{2,1,0:T(2,128)(2,1)S(1)} %reshape.331), channel_id=1, replica_groups=mesh['oct'=2,'sub'=64] {'oct','sub'}, dimensions={0} | all-to-all | bytes 4194304 | tf_op jit(solution)/shard_map/all_to_all | solution.py:141
  772.7 130.4 %all-reduce.5.cloned.1.call-done = f32[128,4096]{1,0:T(8,128)} async-done(((f32[128,4096]{1,0:T(8,128)}), f32[128,4096]{1,0:T(8,128)}) %all-reduce.5.cloned.1.call-update) | async-done | bytes 2097168
  904.7 63.3 %all-gather.7.cloned.1.call-done = bf16[64,2,4096]{2,1,0:T(2,128)(2,1)} async-done(((bf16[1,2,4096]{2,1,0:T(2,128)(2,1)}), bf16[64,2,4096]{2,1,0:T(2,128)(2,1)}) %all-gather.7.cloned.1.call-update) | async-done | bytes 1048592 | tf_op jit(solution)/shard_map/all_gather | solution.py:163
  (182 shorter events, 95.0 us)
Async XLA Ops:
  10.2 16.2 %copy-start.32 = (s32[256,1]{0,1:T(1,128)}, s32[256,1]{0,1:T(1,128)S(1)}, u32[]{:S(2)}) copy-start(s32[256,1]{0,1:T(1,128)S(1)} %compare_select_fusion.1) | copy-start | bytes 3076
  13.1 127.0 %all-to-all-start = ((bf16[128,1,2]{2,1,0:T(2,128)(2,1)}), bf16[128,1,2]{2,1,0:T(2,128)(2,1)}, u32[]{:S(2)}, u32[]{:S(2)}) async-start(bf16[128,1,2]{2,1,0:T(2,128)(2,1)} %all_to_all.17), calls=%async_computation | async-start | bytes 131072 | tf_op jit(solution)/shard_map/all_to_all | solution.py:148
  27.1 98.5 %copy-start.21 = (pred[16,16]{1,0:T(8,128)(4,1)}, pred[16,16]{1,0:T(8,128)(4,1)S(1)}, u32[]{:S(2)}) copy-start(pred[16,16]{1,0:T(8,128)(4,1)S(1)} %and_bitcast_fusion) | copy-start | bytes 772
  34.2 21.4 %copy-start.6 = (f32[256,256,1]{1,0,2:T(8,128)}, f32[256,256,1]{1,0,2:T(8,128)S(1)}, u32[]{:S(2)}) copy-start(f32[256,256,1]{1,0,2:T(8,128)S(1)} %reshape.409) | copy-start | bytes 786436
  140.2 10.0 %copy-start.12 = (f32[2,16,16]{2,1,0:T(8,128)S(1)}, f32[2,16,16]{2,1,0:T(8,128)}, u32[]{:S(2)}) copy-start(f32[2,16,16]{2,1,0:T(8,128)} %param.19) | copy-start | bytes 6148
  140.2 39.8 %all-to-all-start.1 = ((bf16[128,2,4096]{2,1,0:T(2,128)(2,1)}), bf16[128,2,4096]{2,1,0:T(2,128)(2,1)S(1)}, u32[]{:S(2)}, u32[]{:S(2)}) async-start(bf16[128,2,4096]{2,1,0:T(2,128)(2,1)} %reshape.320), calls=%async_computation.1 | async-start | bytes 4194304 | tf_op jit(solution)/shard_map/all_to_all | solution.py:141
  150.1 464.2 %all-gather.5.cloned.1.call-start = ((), (), s32[]{:S(2)}) async-start(), calls=%async_computation.3 | async-start | bytes 1064960 | tf_op jit(solution)/shard_map/all_gather | solution.py:163
  154.6 10.3 %copy-start.35 = (u32[128]{0:T(128)S(1)}, u32[128]{0:T(128)}, u32[]{:S(2)}) copy-start(u32[128]{0:T(128)} %constant.167) | copy-start | bytes 1540
  154.6 11.7 %copy-start.34 = (s32[16]{0:T(128)S(1)}, s32[16]{0:T(128)}, u32[]{:S(2)}) copy-start(s32[16]{0:T(128)} %param.23) | copy-start | bytes 196
  154.6 11.7 %copy-start.33 = (s32[16]{0:T(128)S(1)}, s32[16]{0:T(128)}, u32[]{:S(2)}) copy-start(s32[16]{0:T(128)} %param.22) | copy-start | bytes 196
  164.9 19.3 %copy-start = (f32[1024,256]{1,0:T(8,128)}, f32[1024,256]{1,0:T(8,128)S(1)}, u32[]{:S(2)}) copy-start(f32[1024,256]{1,0:T(8,128)S(1)} %copy.78) | copy-start | bytes 3145732
  166.3 454.5 %copy-start.25 = (pred[16]{0:T(512)(128)(4,1)}, pred[16]{0:T(512)(128)(4,1)S(1)}, u32[]{:S(2)}) copy-start(pred[16]{0:T(512)(128)(4,1)S(1)} %fusion.85) | copy-start | bytes 52
  166.4 402.0 %copy-start.30 = (s32[16]{0:T(128)}, s32[16]{0:T(128)S(1)}, u32[]{:S(2)}) copy-start(s32[16]{0:T(128)S(1)} %get-tuple-element.37) | copy-start | bytes 196
  166.4 450.6 %copy-start.28 = (pred[16]{0:T(512)(128)(4,1)}, pred[16]{0:T(512)(128)(4,1)S(1)}, u32[]{:S(2)}) copy-start(pred[16]{0:T(512)(128)(4,1)S(1)} %get-tuple-element.36) | copy-start | bytes 52
  166.5 20.5 %copy-start.17 = (f32[16,16]{1,0:T(8,128)}, f32[16,16]{1,0:T(8,128)S(1)}, u32[]{:S(2)}) copy-start(f32[16,16]{1,0:T(8,128)S(1)} %get-tuple-element.48) | copy-start | bytes 3076
  166.5 20.5 %copy-start.19 = (f32[16,16]{1,0:T(8,128)}, f32[16,16]{1,0:T(8,128)S(1)}, u32[]{:S(2)}) copy-start(f32[16,16]{1,0:T(8,128)S(1)} %get-tuple-element.49) | copy-start | bytes 3076
  167.7 16.5 %copy-start.23 = (s32[256]{0:T(256)}, s32[256]{0:T(256)S(1)}, u32[]{:S(2)}) copy-start(s32[256]{0:T(256)S(1)} %reshape.335) | copy-start | bytes 3076
  555.3 347.8 %all-reduce.5.cloned.1.call-start = ((), (), s32[]{:S(2)}) async-start(), calls=%async_computation.5 | async-start | bytes 4194304
  568.2 49.9 %copy-start.2 = (f32[1024,256]{1,0:T(8,128)}, f32[1024,256]{1,0:T(8,128)S(1)}, u32[]{:S(2)}) copy-start(f32[1024,256]{1,0:T(8,128)S(1)} %copy.79) | copy-start | bytes 3145732
  568.3 52.6 %copy-start.13 = (f32[16,16]{1,0:T(8,128)}, f32[16,16]{1,0:T(8,128)S(1)}, u32[]{:S(2)}) copy-start(f32[16,16]{1,0:T(8,128)S(1)} %copy.45) | copy-start | bytes 3076
  568.3 52.5 %copy-start.15 = (f32[16,16]{1,0:T(8,128)}, f32[16,16]{1,0:T(8,128)S(1)}, u32[]{:S(2)}) copy-start(f32[16,16]{1,0:T(8,128)S(1)} %copy.46) | copy-start | bytes 3076
  568.4 48.6 %copy-start.27 = (s32[1024]{0:T(1024)}, s32[1024]{0:T(1024)S(1)}, u32[]{:S(2)}) copy-start(s32[1024]{0:T(1024)S(1)} %pad_clamp_fusion) | copy-start | bytes 12292
  772.6 195.3 %all-gather.7.cloned.1.call-start = ((), (), s32[]{:S(2)}) async-start(), calls=%async_computation.4 | async-start | bytes 1064960 | tf_op jit(solution)/shard_map/all_gather | solution.py:163
  904.7 66.5 %copy-start.29 = (pred[16]{0:T(512)(128)(4,1)S(1)}, pred[16]{0:T(512)(128)(4,1)}, u32[]{:S(2)}) copy-start(pred[16]{0:T(512)(128)(4,1)} %copy-done.28) | copy-start | bytes 52
  (17 other events, 51.6 us)
Sparse Core Ops, SparseCore 0:
  555.5 58.7 all-gather.4
  772.7 130.3 all-reduce.4
  906.6 61.3 all-gather.6
where the time goes:
time: 990 us; the launch traced here: 983 us
  blocking collectives  402 us (41%)
  waiting for transfers between devices  252 us (25%)
  local copies, waits for them, and re-layouts  180 us (18%)
  matrix products  85.5 us (9%)
  other arithmetic  26.4 us (3%)
  starting transfers between devices  21.9 us (2%)
  between operations  15.8 us (2%)
    unnamed x1, blocking collectives  366 us
    unnamed x4, waiting for transfers between devices  130 us
    all_gather x2, waiting for transfers between devices, shards(): lax.all_gather(own_parents.astype(jnp.bfloat16), 'sub', axis=0, tiled=True)  109 us
    reshape x2, local copies, waits for them, and re-layouts, convolve(): partial_value.reshape(block_boxes, order_k, term_count, 9 * plane_size)  65.8 us
    dot_general x2, matrix products, convolve(): jnp.dot(source_blk.reshape(block_boxes * order_k, plane_size), yz_kernels...  41.2 us
    all_to_all x1, blocking collectives, shards(): lax.all_to_all(send_tiles.reshape(devices_all, capacity, cube_size), ('oc...  36.1 us
    dot_general x2, matrix products, convolve(): jnp.einsum('bxmr,max->bar', partial_value, x_kernels, preferred_element_t...  23.1 us
  transfers between devices with their start and end apart: 5, of which 4 were waited for; matrix products, arithmetic and copies ran while one was open for 15% of the time, Pallas kernels for 0%

commit v1 on v0

--- a/solution.py
+++ b/solution.py
@@ -160,8 +160,14 @@
         lifted = lift_boxes(gathered, two_scale, lift_quad, child_octant)
         contrib = jnp.dot(member_up, lifted, precision=highest)
         own_parents = lax.psum_scatter(contrib, "sub", scatter_dimension=0, tiled=True)
-        everyone = lax.all_gather(
-            own_parents.astype(jnp.bfloat16), "sub", axis=0, tiled=True
+        everyone = jnp.concatenate(
+            jax.lax.all_to_all(
+                jnp.stack(jax.lax.axis_size("sub") * [own_parents.astype(jnp.bfloat16)], 0),
+                "sub",
+                concat_axis=0,
+                split_axis=0,
+            ),
+            0,
         ).astype(own_parents.dtype)
         matched = jnp.take(everyone, local_parents, axis=0)
         current = gathered - lift_boxes(matched, flipped, drop_quad, child_octant)

time: 990 us -> 916 us (0.925)
  waiting for transfers between devices: 252 us -> 144 us
  blocking collectives: 402 us -> 430 us
    all_gather x2 -> x0, waiting for transfers between devices: 109 us -> none  [shards(): lax.all_gather(own_parents.astype(jnp.bfloat16), 'sub', axis=0, tiled=True)]
    all_to_all x0 -> x1, blocking collectives: none -> 23.1 us  [shards(): jax.lax.all_to_all(jnp.stack(jax.lax.axis_size('sub') * [own_parents.asty...]
    unnamed x4 -> x2, waiting for transfers between devices: 130 us -> 130 us
  transfers between devices with their start and end apart: 5 -> 4, of which waited for: 4 -> 3; matrix products, arithmetic and copies ran while one was open for 15% -> 16% of each run, Pallas kernels for 0% -> 0%
where the time goes in v1:
time: 916 us; the launch traced here: 910 us
  blocking collectives  430 us (47%)
  local copies, waits for them, and re-layouts  181 us (20%)
  waiting for transfers between devices  144 us (16%)
  matrix products  85.5 us (9%)
  starting transfers between devices  27.6 us (3%)
  other arithmetic  26.3 us (3%)
  between operations  15.9 us (2%)
    unnamed x1, blocking collectives  368 us
    unnamed x2, waiting for transfers between devices  130 us
    reshape x2, local copies, waits for them, and re-layouts, convolve(): partial_value.reshape(block_boxes, order_k, term_count, 9 * plane_size)  65.8 us
    dot_general x2, matrix products, convolve(): jnp.dot(source_blk.reshape(block_boxes * order_k, plane_size), yz_kernels...  41.2 us
    all_to_all x1, blocking collectives, shards(): lax.all_to_all(send_tiles.reshape(devices_all, capacity, cube_size), ('oc...  39.2 us
    all_to_all x1, blocking collectives, shards(): jax.lax.all_to_all(jnp.stack(jax.lax.axis_size('sub') * [own_parents.asty...  23.1 us
    dot_general x2, matrix products, convolve(): jnp.einsum('bxmr,max->bar', partial_value, x_kernels, preferred_element_t...  23 us
  transfers between devices with their start and end apart: 4, of which 3 were waited for; matrix products, arithmetic and copies ran while one was open for 16% of the time, Pallas kernels for 0%

profile of v1, /device:TPU:0, one launch (start us, length us, event | category | flops | bytes accessed | tf_op | source)
XLA Modules:
  0.0 909.7 jit_solution(2773843601875598103)
XLA Ops:
  13.1 12.2 %all-to-all-start = ((bf16[128,1,2]{2,1,0:T(2,128)(2,1)}), bf16[128,1,2]{2,1,0:T(2,128)(2,1)}, u32[]{:S(2)}, u32[]{:S(2)}) async-start(bf16[128,1,2]{2,1,0:T(2,128)(2,1)} %all_to_all.25), calls=%async_computation | async-start | bytes 131072 | tf_op jit(solution)/shard_map/all_to_all | solution.py:148
  35.3 20.6 %convolution_convert_fusion.1 = bf16[256,46080]{1,0:T(8,128)(2,1)} fusion(bf16[256,256]{1,0:T(8,128)(2,1)S(1)} %bitcast.217, bf16[256,46080]{1,0:T(8,128)(2,1)} %param.18), kind=kOutput, calls=%fused_computation.8 | convolution fusion | flops 6051594240 | bytes 47316992 | tf_op jit(solution)/shard_map/while/body/eval_jaxpr/dot_general | solution.py:101
  55.9 32.9 %reshape.326 = bf16[16,16,20,2304]{3,2,1,0:T(8,128)(2,1)} reshape(bf16[256,46080]{1,0:T(8,128)(2,1)} %convolution_convert_fusion.1) | data formatting | bytes 47185920 | tf_op jit(solution)/shard_map/while/body/eval_jaxpr/reshape | solution.py:106
  88.8 11.5 %convolution_bitcast_fusion.1 = bf16[16,48,2304]{2,1,0:T(8,128)(2,1)S(1)} fusion(bf16[16,16,20,2304]{3,2,1,0:T(8,128)(2,1)} %reshape.326, bf16[20,48,16]{1,2,0:T(8,128)(2,1)} %param.17), kind=kOutput, calls=%fused_computation.12 | convolution fusion | flops 1132462080 | bytes 27162624 | tf_op jit(solution)/shard_map/while/body/eval_jaxpr/bxmr,max->bar/dot_general | solution.py:107
  105.2 6.0 copy.44
  111.2 5.3 reshape.328
  117.3 8.5 gather_fusion
  129.3 5.1 scatter_custom_fusion.1
  140.3 9.9 %all-to-all-start.1 = ((bf16[128,2,4096]{2,1,0:T(2,128)(2,1)}), bf16[128,2,4096]{2,1,0:T(2,128)(2,1)S(1)}, u32[]{:S(2)}, u32[]{:S(2)}) async-start(bf16[128,2,4096]{2,1,0:T(2,128)(2,1)} %reshape.330), calls=%async_computation.1 | async-start | bytes 4194304 | tf_op jit(solution)/shard_map/all_to_all | solution.py:141
  154.7 8.7 reshape.332
  167.8 12.3 %all-to-all-done.1 = bf16[128,2,4096]{2,1,0:T(2,128)(2,1)S(1)} async-done(((bf16[128,2,4096]{2,1,0:T(2,128)(2,1)}), bf16[128,2,4096]{2,1,0:T(2,128)(2,1)S(1)}, u32[]{:S(2)}, u32[]{:S(2)}) %all-to-all-start.1) | async-done | bytes 2097184 | tf_op jit(solution)/shard_map/all_to_all | solution.py:141
  188.7 367.6 %all-reduce.6 = bf16[128,4096]{1,0:T(8,128)(2,1)S(1)} all-reduce(f32[128,4096]{1,0:T(8,128)S(1)} %fusion.55), channel_id=2, replica_groups=mesh['oct'=2,'sub'=64] {'sub'}, use_global_device_ids=true, to_apply=%region_5.7.clone | all-reduce | flops 524288 | bytes 3145728
  558.3 5.5 all-to-all-start.2
  568.3 8.2 reshape.334
  587.3 20.6 %convolution_convert_fusion = bf16[256,46080]{1,0:T(8,128)(2,1)} fusion(bf16[256,256]{1,0:T(8,128)(2,1)S(1)} %bitcast.218, bf16[256,46080]{1,0:T(8,128)(2,1)} %param.18), kind=kOutput, calls=%fused_computation.7 | convolution fusion | flops 6051594240 | bytes 47316992 | tf_op jit(solution)/shard_map/while/body/eval_jaxpr/dot_general | solution.py:101
  607.9 32.9 %reshape.337 = bf16[16,16,20,2304]{3,2,1,0:T(8,128)(2,1)} reshape(bf16[256,46080]{1,0:T(8,128)(2,1)} %convolution_convert_fusion) | data formatting | bytes 47185920 | tf_op jit(solution)/shard_map/while/body/eval_jaxpr/reshape | solution.py:106
  640.8 11.5 %convolution_bitcast_fusion = bf16[16,48,2304]{2,1,0:T(8,128)(2,1)S(1)} fusion(bf16[16,16,20,2304]{3,2,1,0:T(8,128)(2,1)} %reshape.337, bf16[20,48,16]{1,2,0:T(8,128)(2,1)} %param.17), kind=kOutput, calls=%fused_computation.11 | convolution fusion | flops 1132462080 | bytes 27162624 | tf_op jit(solution)/shard_map/while/body/eval_jaxpr/bxmr,max->bar/dot_general | solution.py:107
  657.4 6.0 copy.55
  663.4 5.1 reshape.339
  668.5 8.5 gather_fusion.2
  680.5 5.3 scatter_custom_fusion.2
  690.4 39.2 %all_to_all.31 = bf16[128,2,4096]{2,1,0:T(2,128)(2,1)} all-to-all(bf16[128,2,4096]{2,1,0:T(2,128)(2,1)S(1)} %reshape.341), channel_id=1, replica_groups=mesh['oct'=2,'sub'=64] {'oct','sub'}, dimensions={0} | all-to-all | bytes 4194304 | tf_op jit(solution)/shard_map/all_to_all | solution.py:141
  739.3 130.5 %all-reduce.5.cloned.1.call-done = f32[128,4096]{1,0:T(8,128)} async-done(((f32[128,4096]{1,0:T(8,128)}), f32[128,4096]{1,0:T(8,128)}) %all-reduce.5.cloned.1.call-update) | async-done | bytes 2097168
  872.3 23.1 %all_to_all.32 = bf16[64,2,4096]{2,1,0:T(2,128)(2,1)S(1)} all-to-all(bf16[64,2,4096]{2,1,0:T(2,128)(2,1)S(1)} %stack.5), channel_id=1, replica_groups=mesh['oct'=2,'sub'=64] {'sub'}, dimensions={0} | all-to-all | bytes 2097152 | tf_op jit(solution)/shard_map/all_to_all | solution.py:164
  (181 shorter events, 96.6 us)
Async XLA Ops:
  10.2 16.5 %copy-start.32 = (s32[256,1]{0,1:T(1,128)}, s32[256,1]{0,1:T(1,128)S(1)}, u32[]{:S(2)}) copy-start(s32[256,1]{0,1:T(1,128)S(1)} %compare_select_fusion.1) | copy-start | bytes 3076
  13.1 127.2 %all-to-all-start = ((bf16[128,1,2]{2,1,0:T(2,128)(2,1)}), bf16[128,1,2]{2,1,0:T(2,128)(2,1)}, u32[]{:S(2)}, u32[]{:S(2)}) async-start(bf16[128,1,2]{2,1,0:T(2,128)(2,1)} %all_to_all.25), calls=%async_computation | async-start | bytes 131072 | tf_op jit(solution)/shard_map/all_to_all | solution.py:148
  27.4 98.4 %copy-start.21 = (pred[16,16]{1,0:T(8,128)(4,1)}, pred[16,16]{1,0:T(8,128)(4,1)S(1)}, u32[]{:S(2)}) copy-start(pred[16,16]{1,0:T(8,128)(4,1)S(1)} %and_bitcast_fusion) | copy-start | bytes 772
  34.5 21.4 %copy-start.6 = (f32[256,256,1]{1,0,2:T(8,128)}, f32[256,256,1]{1,0,2:T(8,128)S(1)}, u32[]{:S(2)}) copy-start(f32[256,256,1]{1,0,2:T(8,128)S(1)} %reshape.415) | copy-start | bytes 786436
  140.3 9.9 %copy-start.12 = (f32[2,16,16]{2,1,0:T(8,128)S(1)}, f32[2,16,16]{2,1,0:T(8,128)}, u32[]{:S(2)}) copy-start(f32[2,16,16]{2,1,0:T(8,128)} %param.19) | copy-start | bytes 6148
  140.3 39.8 %all-to-all-start.1 = ((bf16[128,2,4096]{2,1,0:T(2,128)(2,1)}), bf16[128,2,4096]{2,1,0:T(2,128)(2,1)S(1)}, u32[]{:S(2)}, u32[]{:S(2)}) async-start(bf16[128,2,4096]{2,1,0:T(2,128)(2,1)} %reshape.330), calls=%async_computation.1 | async-start | bytes 4194304 | tf_op jit(solution)/shard_map/all_to_all | solution.py:141
  154.7 10.3 %copy-start.35 = (u32[128]{0:T(128)S(1)}, u32[128]{0:T(128)}, u32[]{:S(2)}) copy-start(u32[128]{0:T(128)} %constant.167) | copy-start | bytes 1540
  154.7 11.7 %copy-start.34 = (s32[16]{0:T(128)S(1)}, s32[16]{0:T(128)}, u32[]{:S(2)}) copy-start(s32[16]{0:T(128)} %param.23) | copy-start | bytes 196
  154.7 11.7 %copy-start.33 = (s32[16]{0:T(128)S(1)}, s32[16]{0:T(128)}, u32[]{:S(2)}) copy-start(s32[16]{0:T(128)} %param.22) | copy-start | bytes 196
  165.0 19.4 %copy-start = (f32[1024,256]{1,0:T(8,128)}, f32[1024,256]{1,0:T(8,128)S(1)}, u32[]{:S(2)}) copy-start(f32[1024,256]{1,0:T(8,128)S(1)} %copy.78) | copy-start | bytes 3145732
  166.4 418.2 %copy-start.25 = (pred[16]{0:T(512)(128)(4,1)}, pred[16]{0:T(512)(128)(4,1)S(1)}, u32[]{:S(2)}) copy-start(pred[16]{0:T(512)(128)(4,1)S(1)} %fusion.84) | copy-start | bytes 52
  166.5 410.6 %copy-start.30 = (s32[16]{0:T(128)}, s32[16]{0:T(128)S(1)}, u32[]{:S(2)}) copy-start(s32[16]{0:T(128)S(1)} %get-tuple-element.37) | copy-start | bytes 196
  166.5 414.2 %copy-start.28 = (pred[16]{0:T(512)(128)(4,1)}, pred[16]{0:T(512)(128)(4,1)S(1)}, u32[]{:S(2)}) copy-start(pred[16]{0:T(512)(128)(4,1)S(1)} %get-tuple-element.36) | copy-start | bytes 52
  166.6 20.5 %copy-start.17 = (f32[16,16]{1,0:T(8,128)}, f32[16,16]{1,0:T(8,128)S(1)}, u32[]{:S(2)}) copy-start(f32[16,16]{1,0:T(8,128)S(1)} %get-tuple-element.48) | copy-start | bytes 3076
  166.6 20.5 %copy-start.19 = (f32[16,16]{1,0:T(8,128)}, f32[16,16]{1,0:T(8,128)S(1)}, u32[]{:S(2)}) copy-start(f32[16,16]{1,0:T(8,128)S(1)} %get-tuple-element.49) | copy-start | bytes 3076
  167.8 16.5 %copy-start.23 = (s32[256]{0:T(256)}, s32[256]{0:T(256)S(1)}, u32[]{:S(2)}) copy-start(s32[256]{0:T(256)S(1)} %reshape.345) | copy-start | bytes 3076
  558.3 19.7 %all-to-all-start.2 = ((bf16[64,2,4096]{2,1,0:T(2,128)(2,1)}), bf16[64,2,4096]{2,1,0:T(2,128)(2,1)}, u32[]{:S(2)}, u32[]{:S(2)}) async-start(bf16[64,2,4096]{2,1,0:T(2,128)(2,1)} %stack.4), calls=%async_computation.2 | async-start | bytes 2097152 | tf_op jit(solution)/shard_map/all_to_all | solution.py:164
  563.8 305.9 %all-reduce.5.cloned.1.call-start = ((), (), s32[]{:S(2)}) async-start(), calls=%async_computation.5 | async-start | bytes 4194304
  576.9 4.9 copy-start.2
  577.0 7.6 copy-start.13
  577.1 7.6 copy-start.15
  577.1 3.6 copy-start.27
  668.5 8.5 copy-start.22
  732.8 3.6 copy-start.26
  (16 other events, 41.4 us)
Sparse Core Ops, SparseCore 0:
  739.4 130.2 all-reduce.4
